TPU v7x, 32 devices: a whole 2x2x4 slice. The times are simulated.
32 devices in a mesh: mem: 4 (over z), gx: 4 (over y, core), gy: 2 (over x).
Axes of the slice: x: 2, y: 2, z: 4, core: 2. Of those that a mesh axis runs over, the one named last changes fastest.
Arguments:
- height: float32 [4, 4, 128, 256], P('mem', None, 'gx', 'gy'), may hold values from -4 to 4
- wind: float32 [4, 2, 4, 128, 256], P('mem', None, None, 'gx', 'gy'), may hold values from -0.8 to 0.8
- moisture: float32 [4, 4, 128, 256], P('mem', None, 'gx', 'gy'), may hold values from 0 to 2
- coeffs: float32 [4, 4, 4, 16384], P('mem', None, None, ('gx', 'gy')), may hold values from -6 to 6
- damping: float32 [16384], P(('gx', 'gy')), may hold values from 0.3 to 1
- vmix: float32 [4, 4], replicated, may hold values from -3 to 3
- basis: bfloat16 [16384, 384], P(('gx', 'gy')), may hold values from -0.046875 to 0.046875
- edge_source: int32 [768], replicated, may hold values from 0 to 383
- row_cell: int32 [128], replicated, may hold values from 0 to 15, never falling along the last dimension, each value on 1 to 16 neighbouring positions
- col_cell: int32 [256], replicated, may hold values from 0 to 31, never falling along the last dimension, each value on 1 to 16 neighbouring positions
- cond_rate: float32 [4], replicated, may hold values from 0.05 to 0.5
- saturation: float32 [4], replicated, may hold values from 0.5 to 1.5
- ancestry: int32 [4], replicated, may hold values from 0 to 3
Outputs:
- height_out: float32 [4, 4, 128, 256], P('mem', None, 'gx', 'gy')
- wind_out: float32 [4, 2, 4, 128, 256], P('mem', None, None, 'gx', 'gy')
- moisture_out: float32 [4, 4, 128, 256], P('mem', None, 'gx', 'gy')
- rainfall: float32 [4, 128, 256], P('mem', 'gx', 'gy')
- restricted: float32 [4, 4, 16, 32], P('mem')
- coeffs_out: float32 [4, 4, 4, 16384], P('mem', None, None, ('gx', 'gy'))
Inputs may be any that keep to these rules, and one draw needn't show every extreme that they name: row_cell never falls, and each of the 16 global rows holds 1 to 16 nest rows, one exactly 16. col_cell never falls, and each of the 32 global columns holds 1 to 16 nest columns, one exactly 16.
All inputs are finite; a program needn't handle non-finite values.
Results may differ from a plain program's by a relative error of at most 0.00035.
Values sent between devices are 32-bit elements; how exact they have to be, the bound alone decides.
A program may use at most 64 MiB of HBM per device.

v0:
```python
import jax
import jax.numpy as jnp
from jax import lax
from jax.sharding import PartitionSpec as P

RATIO = 8
ACOUSTIC = 2
acoustic_substep = 0.2
drift_step = 0.4


def extended(block, sides, width):
    for axis, dim in sides:
        count = lax.axis_size(axis)
        forward = [(i, i + 1) for i in range(count - 1)]
        backward = [(target, source) for source, target in forward]
        low = lax.ppermute(
            lax.slice_in_dim(block, block.shape[dim] - width, None, axis=dim), axis, forward
        )
        high = lax.ppermute(lax.slice_in_dim(block, 0, width, axis=dim), axis, backward)
        block = jnp.concatenate([low, block, high], axis=dim)
    return block


def side_values(rim, indices, rim_points, levels):
    table = (indices[None, :] == lax.iota(jnp.int32, rim_points)[:, None]).astype(jnp.float32)
    return jnp.dot(rim, table, precision=lax.Precision.HIGHEST).reshape(4, levels, indices.shape[0])


def frame(padded, sides, flags):
    western_edge, eastern_edge, southern_edge, northern_edge = sides
    at_west, at_east, at_south, at_north = flags
    size_x = padded.shape[2] - 2
    size_y = padded.shape[3] - 2
    current = padded[:, :, 0, 1 : 1 + size_y]
    padded = padded.at[:, :, 0, 1 : 1 + size_y].set(jnp.where(at_west, western_edge, current))
    current = padded[:, :, 1 + size_x, 1 : 1 + size_y]
    padded = padded.at[:, :, 1 + size_x, 1 : 1 + size_y].set(
        jnp.where(at_east, eastern_edge, current)
    )
    current = padded[:, :, 1 : 1 + size_x, 0]
    padded = padded.at[:, :, 1 : 1 + size_x, 0].set(jnp.where(at_south, southern_edge, current))
    current = padded[:, :, 1 : 1 + size_x, 1 + size_y]
    padded = padded.at[:, :, 1 : 1 + size_x, 1 + size_y].set(
        jnp.where(at_north, northern_edge, current)
    )
    return padded


def pick_sides(sides, first, last):
    return tuple((side[first:last] for side in sides))


def body(
    height,
    wind,
    moisture,
    coeffs,
    damping,
    vmix,
    basis,
    edge_source,
    row_cell,
    col_cell,
    cond_rate,
    saturation,
    ancestry,
):
    levels = height.shape[1]
    size_x = height.shape[2]
    size_y = height.shape[3]
    full_x = row_cell.shape[0]
    full_y = col_cell.shape[0]
    rim_points = basis.shape[1]
    row_index = lax.axis_index("gx")
    col_index = lax.axis_index("gy")
    row_start = row_index * size_x
    col_start = col_index * size_y
    coeff_new = jnp.einsum("lj,mfjk->mflk", vmix, coeffs, precision=lax.Precision.HIGHEST) * damping
    coeff_low = coeff_new.astype(jnp.bfloat16).reshape(4 * levels, -1)
    rim_part = jnp.dot(coeff_low, basis, preferred_element_type=jnp.float32)
    rim = lax.psum(rim_part, ("gx", "gy"))
    western_edge = side_values(
        rim, lax.dynamic_slice_in_dim(edge_source, col_start, size_y), rim_points, levels
    )
    eastern_edge = side_values(
        rim, lax.dynamic_slice_in_dim(edge_source, full_y + col_start, size_y), rim_points, levels
    )
    southern_edge = side_values(
        rim,
        lax.dynamic_slice_in_dim(edge_source, 2 * full_y + row_start, size_x),
        rim_points,
        levels,
    )
    northern_edge = side_values(
        rim,
        lax.dynamic_slice_in_dim(edge_source, 2 * full_y + full_x + row_start, size_x),
        rim_points,
        levels,
    )
    sides = (western_edge, eastern_edge, southern_edge, northern_edge)
    flags = (
        row_index == 0,
        row_index == lax.axis_size("gx") - 1,
        col_index == 0,
        col_index == lax.axis_size("gy") - 1,
    )
    h_field = height[0]
    u_field = wind[0, 0]
    v_field = wind[0, 1]
    q_field = moisture[0]
    for substep in range(ACOUSTIC):
        h_pad = extended(h_field[None], (("gx", 2), ("gy", 3)), 1)
        h_pad = frame(h_pad, pick_sides(sides, 0, 1), flags)[0]
        u_field = u_field - acoustic_substep * (h_pad[:, 2:, 1:-1] - h_pad[:, :-2, 1:-1])
        v_field = v_field - acoustic_substep * (h_pad[:, 1:-1, 2:] - h_pad[:, 1:-1, :-2])
        wind_pad = extended(jnp.stack([u_field, v_field]), (("gx", 2), ("gy", 3)), 1)
        wind_pad = frame(wind_pad, pick_sides(sides, 1, 3), flags)
        u_pad = wind_pad[0]
        v_pad = wind_pad[1]
        h_field = h_field - acoustic_substep * (
            u_pad[:, 2:, 1:-1] - u_pad[:, :-2, 1:-1] + (v_pad[:, 1:-1, 2:] - v_pad[:, 1:-1, :-2])
        )
    q_pad = extended(q_field[None], (("gx", 2), ("gy", 3)), 1)
    q_pad = frame(q_pad, pick_sides(sides, 3, 4), flags)[0]
    flux = (
        jnp.maximum(u_field, 0.0) * (q_field - q_pad[:, :-2, 1:-1])
        + jnp.minimum(u_field, 0.0) * (q_pad[:, 2:, 1:-1] - q_field)
        + (
            jnp.maximum(v_field, 0.0) * (q_field - q_pad[:, 1:-1, :-2])
            + jnp.minimum(v_field, 0.0) * (q_pad[:, 1:-1, 2:] - q_field)
        )
    )
    q_field = q_field - drift_step * flux
    excess = jnp.maximum(q_field - saturation[:, None, None], 0.0)
    fallen = cond_rate[:, None, None] * excess
    q_field = q_field - fallen
    rain = jnp.sum(fallen, axis=0)
    coarse_rows = full_x // RATIO
    coarse_cols = full_y // RATIO
    row_table = (row_cell[None, :] == lax.iota(jnp.int32, coarse_rows)[:, None]).astype(jnp.float32)
    col_table = (col_cell[None, :] == lax.iota(jnp.int32, coarse_cols)[:, None]).astype(jnp.float32)
    row_count = jnp.sum(row_table, axis=1)
    col_count = jnp.sum(col_table, axis=1)
    local_rows = lax.dynamic_slice_in_dim(row_table, row_start, size_x, 1)
    local_cols = lax.dynamic_slice_in_dim(col_table, col_start, size_y, 1)
    partial_value = jnp.einsum("ax,lxy->lay", local_rows, q_field, precision=lax.Precision.HIGHEST)
    partial_value = jnp.einsum(
        "lay,by->lab", partial_value, local_cols, precision=lax.Precision.HIGHEST
    )
    sums = lax.psum(partial_value, "gy")
    sums = lax.psum(sums, "gx")
    coarse = sums / (row_count[:, None] * col_count[None, :])
    states = (
        h_field[None],
        jnp.stack([u_field, v_field])[None],
        q_field[None],
        rain[None],
        coarse[None],
        coeff_new,
    )
    member_here = lax.axis_index("mem")
    everyone = (
        lax.all_gather(states[0], "mem", axis=0, tiled=True),
        lax.all_gather(states[1], "mem", axis=0, tiled=True),
        lax.all_gather(states[2], "mem", axis=0, tiled=True),
        lax.all_gather(states[3], "mem", axis=0, tiled=True),
        lax.all_gather(states[4], "mem", axis=0, tiled=True),
        lax.all_gather(states[5], "mem", axis=0, tiled=True),
    )
    source = ancestry[member_here]
    cloned = tuple(
        (lax.dynamic_index_in_dim(whole, source, 0, keepdims=True) for whole in everyone)
    )
    return (cloned[0], cloned[1], cloned[2], cloned[3], cloned[4], cloned[5])


def solution(mesh):
    in_specs = (
        P("mem", None, "gx", "gy"),
        P("mem", None, None, "gx", "gy"),
        P("mem", None, "gx", "gy"),
        P("mem", None, None, ("gx", "gy")),
        P(("gx", "gy")),
        P(),
        P(("gx", "gy"), None),
        P(),
        P(),
        P(),
        P(),
        P(),
        P(),
    )
    out_specs = (
        P("mem", None, "gx", "gy"),
        P("mem", None, None, "gx", "gy"),
        P("mem", None, "gx", "gy"),
        P("mem", "gx", "gy"),
        P("mem", None, None, None),
        P("mem", None, None, ("gx", "gy")),
    )
    return jax.shard_map(body, mesh=mesh, in_specs=in_specs, out_specs=out_specs, check_vma=False)
```

profile of v0, /device:TPU:10, one launch (start us, length us, event | category | flops | bytes accessed | tf_op | source)
XLA Modules:
  0.0 245.4 jit_solution(11485259475965265100)
XLA Ops:
  1.5 1.7 collective-permute-start
  5.3 4.3 %collective-permute-start.16 = (f32[1,4,1,128]{3,1,2,0:T(4,128)S(1)}, f32[1,4,1,128]{3,1,2,0:T(4,128)S(1)}, u32[]{:S(2)}, u32[]{:S(2)}) collective-permute-start(f32[1,4,1,128]{3,1,2,0:T(4,128)S(1)} %copy.119), channel_id=1, source_target_pairs={{0,2},{2,4},{4,6},{1,3},{3,5},{5,7},{8,10},{10,12},{12,14},{9,11},... | collective-permute-start | bytes 6152 | tf_op jit(solution)/shard_map/ppermute | solution.py:17
  18.1 25.0 %psum.21 = f32[16,384]{1,0:T(8,128)S(1)} all-reduce(f32[16,384]{1,0:T(8,128)S(1)} %fusion.78), channel_id=1, replica_groups=mesh['mem'=4,'gx'=4,'gy'=2] {'gx','gy'}, use_global_device_ids=true, to_apply=%region_0.0 | all-reduce | flops 6144 | bytes 49152 | tf_op jit(solution)/shard_map/psum | solution.py:82
  44.0 16.5 %all_gather.23 = f32[4,4,4,2048]{3,2,1,0:T(4,128)S(1)} all-gather(f32[1,4,4,2048]{3,2,1,0:T(4,128)S(1)} %get-tuple-element.293), channel_id=1, replica_groups=mesh['mem'=4,'gx'=4,'gy'=2] {'mem'}, dimensions={0}, use_global_device_ids=true | all-gather | bytes 655360 | tf_op jit(solution)/shard_map/all_gather | solution.py:169
  63.0 3.3 %collective-permute-start.3 = (f32[1,4,34,1]{3,1,2,0:T(4,128)S(1)}, f32[1,4,34,1]{3,1,2,0:T(4,128)S(1)}, u32[]{:S(2)}, u32[]{:S(2)}) collective-permute-start(f32[1,4,34,1]{3,1,2,0:T(4,128)S(1)} %get-tuple-element.271), channel_id=1, source_target_pairs={{1,0},{3,2},{5,4},{7,6},{9,8},{11,10},{13,12},{15,14},{17,16},{19,... | collective-permute-start | bytes 1640 | tf_op jit(solution)/shard_map/ppermute | solution.py:20
  68.2 4.3 %collective-permute-done.2 = f32[1,4,34,1]{3,1,2,0:T(4,128)S(1)} collective-permute-done((f32[1,4,34,1]{3,1,2,0:T(4,128)S(1)}, f32[1,4,34,1]{3,1,2,0:T(4,128)S(1)}, u32[]{:S(2)}, u32[]{:S(2)}) %collective-permute-start.2) | collective-permute-done | bytes 576 | tf_op jit(solution)/shard_map/ppermute | solution.py:17
  75.2 2.4 scatter.71
  79.1 3.0 %collective-permute-start.4 = (f32[2,4,1,128]{3,1,2,0:T(4,128)S(1)}, f32[2,4,1,128]{3,1,2,0:T(4,128)S(1)}, u32[]{:S(2)}, u32[]{:S(2)}) collective-permute-start(f32[2,4,1,128]{3,1,2,0:T(4,128)S(1)} %get-tuple-element.262), channel_id=1, source_target_pairs={{0,2},{2,4},{4,6},{1,3},{3,5},{5,7},{8,10},{10,12},{12,14},{9,11},... | collective-permute-start | bytes 12296 | tf_op jit(solution)/shard_map/ppermute | solution.py:17
  82.3 1.6 collective-permute-start.19
  85.4 4.6 %collective-permute-start.7 = (f32[2,4,34,1]{3,1,2,0:T(4,128)S(1)}, f32[2,4,34,1]{3,1,2,0:T(4,128)S(1)}, u32[]{:S(2)}, u32[]{:S(2)}) collective-permute-start(f32[2,4,34,1]{3,1,2,0:T(4,128)S(1)} %get-tuple-element.257), channel_id=1, source_target_pairs={{1,0},{3,2},{5,4},{7,6},{9,8},{11,10},{13,12},{15,14},{17,16},{19,... | collective-permute-start | bytes 3272 | tf_op jit(solution)/shard_map/ppermute | solution.py:20
  91.2 2.6 %collective-permute-done.7 = f32[2,4,34,1]{3,1,2,0:T(4,128)S(1)} collective-permute-done((f32[2,4,34,1]{3,1,2,0:T(4,128)S(1)}, f32[2,4,34,1]{3,1,2,0:T(4,128)S(1)}, u32[]{:S(2)}, u32[]{:S(2)}) %collective-permute-start.7) | collective-permute-done | bytes 1120 | tf_op jit(solution)/shard_map/ppermute | solution.py:20
  93.8 4.4 %collective-permute-done.6 = f32[2,4,34,1]{3,1,2,0:T(4,128)S(1)} collective-permute-done((f32[2,4,34,1]{3,1,2,0:T(4,128)S(1)}, f32[2,4,34,1]{3,1,2,0:T(4,128)S(1)}, u32[]{:S(2)}, u32[]{:S(2)}) %collective-permute-start.6) | collective-permute-done | bytes 1120 | tf_op jit(solution)/shard_map/ppermute | solution.py:17
  98.5 1.6 scatter.74
  101.3 4.8 %scatter.79 = f32[2,4,34,130]{3,1,2,0:T(4,128)S(1)} dynamic-update-slice(f32[2,4,34,130]{3,1,2,0:T(4,128)S(1)} %scatter.76, f32[2,4,32,1]{3,1,2,0:T(4,128)S(1)} %slice_select_fusion.2, s32[]{:T(128)} %constant.509.clone.1, s32[]{:T(128)} %constant.509.clone.1, s32[]{:T(128)} %constant.516.clone.1, s32[]{:T(128)} %constant.522.clone.1) | dynamic-update-slice | bytes 2052 | tf_op jit(solution)/shard_map/scatter | solution.py:44
  106.3 1.9 collective-permute-start.8
  109.7 1.9 collective-permute-done.9
  116.0 3.4 %collective-permute-done.10 = f32[1,4,34,1]{3,1,2,0:T(4,128)S(1)} collective-permute-done((f32[1,4,34,1]{3,1,2,0:T(4,128)S(1)}, f32[1,4,34,1]{3,1,2,0:T(4,128)S(1)}, u32[]{:S(2)}, u32[]{:S(2)}) %collective-permute-start.10) | collective-permute-done | bytes 576 | tf_op jit(solution)/shard_map/ppermute | solution.py:17
  119.6 1.5 scatter.80
  123.2 2.4 scatter.99
  125.6 2.6 %scatter.85 = f32[4,34,130]{2,0,1:T(4,128)S(1)} dynamic-update-slice(f32[4,34,130]{2,0,1:T(4,128)S(1)} %bitcast.149, f32[4,32,1]{2,0,1:T(4,128)S(1)} %copy.88, s32[]{:T(128)} %constant.509.clone.1, s32[]{:T(128)} %constant.516.clone.1, s32[]{:T(128)} %constant.522.clone.1) | dynamic-update-slice | bytes 1028 | tf_op jit(solution)/shard_map/scatter | solution.py:44
  129.9 3.5 %collective-permute-start.12 = (f32[2,4,1,128]{3,1,2,0:T(4,128)S(1)}, f32[2,4,1,128]{3,1,2,0:T(4,128)S(1)}, u32[]{:S(2)}, u32[]{:S(2)}) collective-permute-start(f32[2,4,1,128]{3,1,2,0:T(4,128)S(1)} %get-tuple-element.260), channel_id=1, source_target_pairs={{0,2},{2,4},{4,6},{1,3},{3,5},{5,7},{8,10},{10,12},{12,14},{9,11},... | collective-permute-start | bytes 12296 | tf_op jit(solution)/shard_map/ppermute | solution.py:17
  133.4 16.1 %all-gather.1 = f32[8,4,32,128]{3,2,1,0:T(8,128)S(1)} all-gather(f32[2,4,32,128]{3,2,1,0:T(8,128)S(1)} %copy.92), channel_id=3, replica_groups=mesh['mem'=4,'gx'=4,'gy'=2] {'mem'}, dimensions={0}, use_global_device_ids=true | all-gather | bytes 655360 | tf_op jit(solution)/shard_map/all_gather | solution.py:165
  150.3 14.7 %all-gather.2 = f32[16,32,128]{2,1,0:T(8,128)S(1)} all-gather(f32[4,32,128]{2,1,0:T(8,128)S(1)} %copy.101), channel_id=4, replica_groups=mesh['mem'=4,'gx'=4,'gy'=2] {'mem'}, dimensions={0}, use_global_device_ids=true | all-gather | bytes 327680 | tf_op jit(solution)/shard_map/all_gather | solution.py:166
  165.7 13.2 %all-gather.3 = f32[128,128]{1,0:T(8,128)S(1)} all-gather(f32[32,128]{1,0:T(8,128)S(1)} %get-tuple-element.246), channel_id=5, replica_groups=mesh['mem'=4,'gx'=4,'gy'=2] {'mem'}, dimensions={0}, use_global_device_ids=true | all-gather | bytes 81920 | tf_op jit(solution)/shard_map/all_gather | solution.py:167
  179.2 7.0 %psum.22 = f32[4,16,32]{2,1,0:T(8,128)S(1)} all-reduce(f32[4,16,32]{2,1,0:T(8,128)S(1)} %fusion.36), channel_id=1, replica_groups=mesh['mem'=4,'gx'=4,'gy'=2] {'gy'}, use_global_device_ids=true, to_apply=%region_2.3 | all-reduce | flops 2048 | bytes 16384 | tf_op jit(solution)/shard_map/psum | solution.py:151
  186.2 10.3 %psum.23 = f32[4,16,32]{2,1,0:T(8,128)S(1)} all-reduce(f32[4,16,32]{2,1,0:T(8,128)S(1)} %psum.22), channel_id=1, replica_groups=mesh['mem'=4,'gx'=4,'gy'=2] {'gx'}, use_global_device_ids=true, to_apply=%region_3.4 | all-reduce | flops 2048 | bytes 16384 | tf_op jit(solution)/shard_map/psum | solution.py:152
  196.5 13.6 %all-gather.4 = f32[16,16,32]{2,1,0:T(8,128)S(1)} all-gather(f32[4,16,32]{2,1,0:T(8,128)S(1)} %broadcast_divide_fusion), channel_id=6, replica_groups=mesh['mem'=4,'gx'=4,'gy'=2] {'mem'}, dimensions={0}, use_global_device_ids=true | all-gather | bytes 40960 | tf_op jit(solution)/shard_map/all_gather | solution.py:168
  211.5 3.8 %collective-permute-start.15 = (f32[2,4,34,1]{3,1,2,0:T(4,128)S(1)}, f32[2,4,34,1]{3,1,2,0:T(4,128)S(1)}, u32[]{:S(2)}, u32[]{:S(2)}) collective-permute-start(f32[2,4,34,1]{3,1,2,0:T(4,128)S(1)} %get-tuple-element.255), channel_id=1, source_target_pairs={{1,0},{3,2},{5,4},{7,6},{9,8},{11,10},{13,12},{15,14},{17,16},{19,... | collective-permute-start | bytes 3272 | tf_op jit(solution)/shard_map/ppermute | solution.py:20
  217.9 4.4 %collective-permute-done.14 = f32[2,4,34,1]{3,1,2,0:T(4,128)S(1)} collective-permute-done((f32[2,4,34,1]{3,1,2,0:T(4,128)S(1)}, f32[2,4,34,1]{3,1,2,0:T(4,128)S(1)}, u32[]{:S(2)}, u32[]{:S(2)}) %collective-permute-start.14) | collective-permute-done | bytes 1120 | tf_op jit(solution)/shard_map/ppermute | solution.py:17
  222.5 1.6 scatter.86
  225.3 4.8 %scatter.91 = f32[2,4,34,130]{3,1,2,0:T(4,128)S(1)} dynamic-update-slice(f32[2,4,34,130]{3,1,2,0:T(4,128)S(1)} %scatter.90, f32[2,4,32,1]{3,1,2,0:T(4,128)S(1)} %slice_select_fusion, s32[]{:T(128)} %constant.509.clone.1, s32[]{:T(128)} %constant.509.clone.1, s32[]{:T(128)} %constant.516.clone.1, s32[]{:T(128)} %constant.522.clone.1) | dynamic-update-slice | bytes 2052 | tf_op jit(solution)/shard_map/scatter | solution.py:44
  230.3 14.4 %all-gather = f32[16,32,128]{2,1,0:T(8,128)S(1)} all-gather(f32[4,32,128]{2,1,0:T(8,128)S(1)} %copy.91), channel_id=2, replica_groups=mesh['mem'=4,'gx'=4,'gy'=2] {'mem'}, dimensions={0}, use_global_device_ids=true | all-gather | bytes 327680 | tf_op jit(solution)/shard_map/all_gather | solution.py:164
  (157 shorter events, 40.8 us)
Async XLA Ops:
  0.6 17.1 %copy-start = (bf16[2048,384]{1,0:T(8,128)(2,1)S(1)}, bf16[2048,384]{1,0:T(8,128)(2,1)}, u32[]{:S(2)}) copy-start(bf16[2048,384]{1,0:T(8,128)(2,1)} %param.59) | copy-start | bytes 4718596
  0.6 42.4 %copy-start.6 = (s32[768]{0:T(1024)S(1)}, s32[768]{0:T(1024)}, u32[]{:S(2)}) copy-start(s32[768]{0:T(1024)} %param.60) | copy-start | bytes 9220
  0.7 43.3 %copy-start.3 = (f32[1,2,4,32,128]{4,3,2,1,0:T(8,128)S(1)}, f32[1,2,4,32,128]{4,3,2,1,0:T(8,128)}, u32[]{:S(2)}) copy-start(f32[1,2,4,32,128]{4,3,2,1,0:T(8,128)} %param.54) | copy-start | bytes 393220
  1.5 61.3 %collective-permute-start = (f32[1,4,1,128]{3,1,2,0:T(4,128)S(1)}, f32[1,4,1,128]{3,1,2,0:T(4,128)S(1)}, u32[]{:S(2)}, u32[]{:S(2)}) collective-permute-start(f32[1,4,1,128]{3,1,2,0:T(4,128)S(1)} %copy.117), channel_id=1, source_target_pairs={{0,2},{2,4},{4,6},{1,3},{3,5},{5,7},{8,10},{10,12},{12,14},{9,11},... | collective-permute-start | bytes 6152 | tf_op jit(solution)/shard_map/ppermute | solution.py:17
  3.3 59.6 %collective-permute-start.1 = (f32[1,4,1,128]{3,1,2,0:T(4,128)S(1)}, f32[1,4,1,128]{3,1,2,0:T(4,128)S(1)}, u32[]{:S(2)}, u32[]{:S(2)}) collective-permute-start(f32[1,4,1,128]{3,1,2,0:T(4,128)S(1)} %copy.118), channel_id=1, source_target_pairs={{2,0},{4,2},{6,4},{3,1},{5,3},{7,5},{10,8},{12,10},{14,12},{11,9},... | collective-permute-start | bytes 6152 | tf_op jit(solution)/shard_map/ppermute | solution.py:20
  5.3 62.2 %collective-permute-start.16 = (f32[1,4,1,128]{3,1,2,0:T(4,128)S(1)}, f32[1,4,1,128]{3,1,2,0:T(4,128)S(1)}, u32[]{:S(2)}, u32[]{:S(2)}) collective-permute-start(f32[1,4,1,128]{3,1,2,0:T(4,128)S(1)} %copy.119), channel_id=1, source_target_pairs={{0,2},{2,4},{4,6},{1,3},{3,5},{5,7},{8,10},{10,12},{12,14},{9,11},... | collective-permute-start | bytes 6152 | tf_op jit(solution)/shard_map/ppermute | solution.py:17
  9.7 58.0 %collective-permute-start.17 = (f32[1,4,1,128]{3,1,2,0:T(4,128)S(1)}, f32[1,4,1,128]{3,1,2,0:T(4,128)S(1)}, u32[]{:S(2)}, u32[]{:S(2)}) collective-permute-start(f32[1,4,1,128]{3,1,2,0:T(4,128)S(1)} %copy.120), channel_id=1, source_target_pairs={{2,0},{4,2},{6,4},{3,1},{5,3},{7,5},{10,8},{12,10},{14,12},{11,9},... | collective-permute-start | bytes 6152 | tf_op jit(solution)/shard_map/ppermute | solution.py:20
  17.8 45.0 %copy-start.2 = (f32[1,4,32,128]{3,2,1,0:T(8,128)S(1)}, f32[1,4,32,128]{3,2,1,0:T(8,128)}, u32[]{:S(2)}) copy-start(f32[1,4,32,128]{3,2,1,0:T(8,128)} %param.53) | copy-start | bytes 196612
  17.8 49.8 %copy-start.1 = (f32[1,4,32,128]{3,2,1,0:T(8,128)S(1)}, f32[1,4,32,128]{3,2,1,0:T(8,128)}, u32[]{:S(2)}) copy-start(f32[1,4,32,128]{3,2,1,0:T(8,128)} %param.55) | copy-start | bytes 196612
  63.0 5.2 %collective-permute-start.3 = (f32[1,4,34,1]{3,1,2,0:T(4,128)S(1)}, f32[1,4,34,1]{3,1,2,0:T(4,128)S(1)}, u32[]{:S(2)}, u32[]{:S(2)}) collective-permute-start(f32[1,4,34,1]{3,1,2,0:T(4,128)S(1)} %get-tuple-element.271), channel_id=1, source_target_pairs={{1,0},{3,2},{5,4},{7,6},{9,8},{11,10},{13,12},{15,14},{17,16},{19,... | collective-permute-start | bytes 1640 | tf_op jit(solution)/shard_map/ppermute | solution.py:20
  66.3 6.2 %collective-permute-start.2 = (f32[1,4,34,1]{3,1,2,0:T(4,128)S(1)}, f32[1,4,34,1]{3,1,2,0:T(4,128)S(1)}, u32[]{:S(2)}, u32[]{:S(2)}) collective-permute-start(f32[1,4,34,1]{3,1,2,0:T(4,128)S(1)} %get-tuple-element.270), channel_id=1, source_target_pairs={{0,1},{2,3},{4,5},{6,7},{8,9},{10,11},{12,13},{14,15},{16,17},{18,... | collective-permute-start | bytes 1640 | tf_op jit(solution)/shard_map/ppermute | solution.py:17
  77.8 7.3 %collective-permute-start.5 = (f32[2,4,1,128]{3,1,2,0:T(4,128)S(1)}, f32[2,4,1,128]{3,1,2,0:T(4,128)S(1)}, u32[]{:S(2)}, u32[]{:S(2)}) collective-permute-start(f32[2,4,1,128]{3,1,2,0:T(4,128)S(1)} %get-tuple-element.263), channel_id=1, source_target_pairs={{2,0},{4,2},{6,4},{3,1},{5,3},{7,5},{10,8},{12,10},{14,12},{11,9},... | collective-permute-start | bytes 12296 | tf_op jit(solution)/shard_map/ppermute | solution.py:20
  79.1 6.0 %collective-permute-start.4 = (f32[2,4,1,128]{3,1,2,0:T(4,128)S(1)}, f32[2,4,1,128]{3,1,2,0:T(4,128)S(1)}, u32[]{:S(2)}, u32[]{:S(2)}) collective-permute-start(f32[2,4,1,128]{3,1,2,0:T(4,128)S(1)} %get-tuple-element.262), channel_id=1, source_target_pairs={{0,2},{2,4},{4,6},{1,3},{3,5},{5,7},{8,10},{10,12},{12,14},{9,11},... | collective-permute-start | bytes 12296 | tf_op jit(solution)/shard_map/ppermute | solution.py:17
  82.3 27.3 %collective-permute-start.19 = (f32[1,4,34,1]{3,1,2,0:T(4,128)S(1)}, f32[1,4,34,1]{3,1,2,0:T(4,128)S(1)}, u32[]{:S(2)}, u32[]{:S(2)}) collective-permute-start(f32[1,4,34,1]{3,1,2,0:T(4,128)S(1)} %get-tuple-element.267), channel_id=1, source_target_pairs={{1,0},{3,2},{5,4},{7,6},{9,8},{11,10},{13,12},{15,14},{17,16},{19,... | collective-permute-start | bytes 1640 | tf_op jit(solution)/shard_map/ppermute | solution.py:20
  83.9 25.7 %collective-permute-start.18 = (f32[1,4,34,1]{3,1,2,0:T(4,128)S(1)}, f32[1,4,34,1]{3,1,2,0:T(4,128)S(1)}, u32[]{:S(2)}, u32[]{:S(2)}) collective-permute-start(f32[1,4,34,1]{3,1,2,0:T(4,128)S(1)} %get-tuple-element.266), channel_id=1, source_target_pairs={{0,1},{2,3},{4,5},{6,7},{8,9},{10,11},{12,13},{14,15},{16,17},{18,... | collective-permute-start | bytes 1640 | tf_op jit(solution)/shard_map/ppermute | solution.py:17
  85.4 8.4 %collective-permute-start.7 = (f32[2,4,34,1]{3,1,2,0:T(4,128)S(1)}, f32[2,4,34,1]{3,1,2,0:T(4,128)S(1)}, u32[]{:S(2)}, u32[]{:S(2)}) collective-permute-start(f32[2,4,34,1]{3,1,2,0:T(4,128)S(1)} %get-tuple-element.257), channel_id=1, source_target_pairs={{1,0},{3,2},{5,4},{7,6},{9,8},{11,10},{13,12},{15,14},{17,16},{19,... | collective-permute-start | bytes 3272 | tf_op jit(solution)/shard_map/ppermute | solution.py:20
  89.9 8.3 %collective-permute-start.6 = (f32[2,4,34,1]{3,1,2,0:T(4,128)S(1)}, f32[2,4,34,1]{3,1,2,0:T(4,128)S(1)}, u32[]{:S(2)}, u32[]{:S(2)}) collective-permute-start(f32[2,4,34,1]{3,1,2,0:T(4,128)S(1)} %get-tuple-element.256), channel_id=1, source_target_pairs={{0,1},{2,3},{4,5},{6,7},{8,9},{10,11},{12,13},{14,15},{16,17},{18,... | collective-permute-start | bytes 3272 | tf_op jit(solution)/shard_map/ppermute | solution.py:17
  106.1 22.1 %copy-start.4 = (f32[4]{0:T(128)S(1)}, f32[4]{0:T(128)}, u32[]{:S(2)}) copy-start(f32[4]{0:T(128)} %param.64) | copy-start | bytes 52
  106.1 22.1 %copy-start.5 = (f32[4]{0:T(128)S(1)}, f32[4]{0:T(128)}, u32[]{:S(2)}) copy-start(f32[4]{0:T(128)} %param.63) | copy-start | bytes 52
  106.3 3.4 %collective-permute-start.8 = (f32[1,4,1,128]{3,1,2,0:T(4,128)S(1)}, f32[1,4,1,128]{3,1,2,0:T(4,128)S(1)}, u32[]{:S(2)}, u32[]{:S(2)}) collective-permute-start(f32[1,4,1,128]{3,1,2,0:T(4,128)S(1)} %get-tuple-element.274), channel_id=1, source_target_pairs={{0,2},{2,4},{4,6},{1,3},{3,5},{5,7},{8,10},{10,12},{12,14},{9,11},... | collective-permute-start | bytes 6152 | tf_op jit(solution)/shard_map/ppermute | solution.py:17
  108.2 3.4 %collective-permute-start.9 = (f32[1,4,1,128]{3,1,2,0:T(4,128)S(1)}, f32[1,4,1,128]{3,1,2,0:T(4,128)S(1)}, u32[]{:S(2)}, u32[]{:S(2)}) collective-permute-start(f32[1,4,1,128]{3,1,2,0:T(4,128)S(1)} %get-tuple-element.275), channel_id=1, source_target_pairs={{2,0},{4,2},{6,4},{3,1},{5,3},{7,5},{10,8},{12,10},{14,12},{11,9},... | collective-permute-start | bytes 6152 | tf_op jit(solution)/shard_map/ppermute | solution.py:20
  111.7 4.3 %collective-permute-start.11 = (f32[1,4,34,1]{3,1,2,0:T(4,128)S(1)}, f32[1,4,34,1]{3,1,2,0:T(4,128)S(1)}, u32[]{:S(2)}, u32[]{:S(2)}) collective-permute-start(f32[1,4,34,1]{3,1,2,0:T(4,128)S(1)} %get-tuple-element.269), channel_id=1, source_target_pairs={{1,0},{3,2},{5,4},{7,6},{9,8},{11,10},{13,12},{15,14},{17,16},{19,... | collective-permute-start | bytes 1640 | tf_op jit(solution)/shard_map/ppermute | solution.py:20
  113.2 6.2 %collective-permute-start.10 = (f32[1,4,34,1]{3,1,2,0:T(4,128)S(1)}, f32[1,4,34,1]{3,1,2,0:T(4,128)S(1)}, u32[]{:S(2)}, u32[]{:S(2)}) collective-permute-start(f32[1,4,34,1]{3,1,2,0:T(4,128)S(1)} %get-tuple-element.268), channel_id=1, source_target_pairs={{0,1},{2,3},{4,5},{6,7},{8,9},{10,11},{12,13},{14,15},{16,17},{18,... | collective-permute-start | bytes 1640 | tf_op jit(solution)/shard_map/ppermute | solution.py:17
  128.6 82.7 %collective-permute-start.13 = (f32[2,4,1,128]{3,1,2,0:T(4,128)S(1)}, f32[2,4,1,128]{3,1,2,0:T(4,128)S(1)}, u32[]{:S(2)}, u32[]{:S(2)}) collective-permute-start(f32[2,4,1,128]{3,1,2,0:T(4,128)S(1)} %get-tuple-element.261), channel_id=1, source_target_pairs={{2,0},{4,2},{6,4},{3,1},{5,3},{7,5},{10,8},{12,10},{14,12},{11,9},... | collective-permute-start | bytes 12296 | tf_op jit(solution)/shard_map/ppermute | solution.py:20
  129.9 81.4 %collective-permute-start.12 = (f32[2,4,1,128]{3,1,2,0:T(4,128)S(1)}, f32[2,4,1,128]{3,1,2,0:T(4,128)S(1)}, u32[]{:S(2)}, u32[]{:S(2)}) collective-permute-start(f32[2,4,1,128]{3,1,2,0:T(4,128)S(1)} %get-tuple-element.260), channel_id=1, source_target_pairs={{0,2},{2,4},{4,6},{1,3},{3,5},{5,7},{8,10},{10,12},{12,14},{9,11},... | collective-permute-start | bytes 12296 | tf_op jit(solution)/shard_map/ppermute | solution.py:17
  211.5 6.4 %collective-permute-start.15 = (f32[2,4,34,1]{3,1,2,0:T(4,128)S(1)}, f32[2,4,34,1]{3,1,2,0:T(4,128)S(1)}, u32[]{:S(2)}, u32[]{:S(2)}) collective-permute-start(f32[2,4,34,1]{3,1,2,0:T(4,128)S(1)} %get-tuple-element.255), channel_id=1, source_target_pairs={{1,0},{3,2},{5,4},{7,6},{9,8},{11,10},{13,12},{15,14},{17,16},{19,... | collective-permute-start | bytes 3272 | tf_op jit(solution)/shard_map/ppermute | solution.py:20
  215.3 6.9 %collective-permute-start.14 = (f32[2,4,34,1]{3,1,2,0:T(4,128)S(1)}, f32[2,4,34,1]{3,1,2,0:T(4,128)S(1)}, u32[]{:S(2)}, u32[]{:S(2)}) collective-permute-start(f32[2,4,34,1]{3,1,2,0:T(4,128)S(1)} %get-tuple-element.254), channel_id=1, source_target_pairs={{0,1},{2,3},{4,5},{6,7},{8,9},{10,11},{12,13},{14,15},{16,17},{18,... | collective-permute-start | bytes 3272 | tf_op jit(solution)/shard_map/ppermute | solution.py:17
where the time goes:
time: 246 us; the launch traced here: 245 us
  blocking collectives  131 us (53%)
  starting transfers between devices  42.1 us (17%)
  local copies, waits for them, and re-layouts  37.8 us (15%)
  waiting for transfers between devices  22.7 us (9%)
  other arithmetic  5.81 us (2%)
  between operations  3.52 us (1%)
  matrix products  2.68 us (1%)
    psum x1, blocking collectives, body(): rim = lax.psum(rim_part, ('gx', 'gy'))  25 us
    ppermute x10, starting transfers between devices, extended(): lax.ppermute(lax.slice_in_dim(block, 0, width, axis=dim), axis, backward)  21.2 us
    ppermute x10, starting transfers between devices, extended(): lax.ppermute(lax.slice_in_dim(block, block.shape[dim] - width, None, axis...  21 us
    scatter x5, local copies, waits for them, and re-layouts, frame(): padded.at[:, :, 1:1 + size_x, 1 + size_y]  16.9 us
    ppermute x10, waiting for transfers between devices, extended(): lax.ppermute(lax.slice_in_dim(block, block.shape[dim] - width, None, axis...  16.5 us
    all_gather x1, blocking collectives, body(): lax.all_gather(states[5], 'mem', axis=0, tiled=True)  16.5 us
    all_gather x1, blocking collectives, body(): lax.all_gather(states[1], 'mem', axis=0, tiled=True)  16.1 us
    all_gather x1, blocking collectives, body(): lax.all_gather(states[2], 'mem', axis=0, tiled=True)  14.7 us
  transfers between devices with their start and end apart: 20, of which 8 were waited for; matrix products, arithmetic and copies ran while one was open for 9% of the time, Pallas kernels for 0%

commit v1 on v0

--- a/solution.py
+++ b/solution.py
@@ -79,7 +79,7 @@
     coeff_new = jnp.einsum("lj,mfjk->mflk", vmix, coeffs, precision=lax.Precision.HIGHEST) * damping
     coeff_low = coeff_new.astype(jnp.bfloat16).reshape(4 * levels, -1)
     rim_part = jnp.dot(coeff_low, basis, preferred_element_type=jnp.float32)
-    rim = lax.psum(rim_part, ("gx", "gy"))
+    rim = jnp.sum(lax.all_gather(rim_part, ("gx", "gy")), axis=0)
     western_edge = side_values(
         rim, lax.dynamic_slice_in_dim(edge_source, col_start, size_y), rim_points, levels
     )

time: 246 us -> 238 us (0.967)
  blocking collectives: 131 us -> 122 us
    psum x1 -> x0, blocking collectives: 25 us -> none  [body(): rim = lax.psum(rim_part, ('gx', 'gy'))]
    all_gather x0 -> x1, blocking collectives: none -> 17.2 us  [body(): rim = jnp.sum(lax.all_gather(rim_part, ('gx', 'gy')), axis=0)]
where the time goes in v1:
time: 238 us; the launch traced here: 237 us
  blocking collectives  122 us (51%)
  starting transfers between devices  42.3 us (18%)
  local copies, waits for them, and re-layouts  37.8 us (16%)
  waiting for transfers between devices  22.7 us (10%)
  other arithmetic  5.82 us (2%)
  between operations  3.53 us (1%)
  matrix products  2.68 us (1%)
    ppermute x10, starting transfers between devices, extended(): lax.ppermute(lax.slice_in_dim(block, 0, width, axis=dim), axis, backward)  21.5 us
    ppermute x10, starting transfers between devices, extended(): lax.ppermute(lax.slice_in_dim(block, block.shape[dim] - width, None, axis...  20.7 us
    all_gather x1, blocking collectives, body(): rim = jnp.sum(lax.all_gather(rim_part, ('gx', 'gy')), axis=0)  17.2 us
    scatter x5, local copies, waits for them, and re-layouts, frame(): padded.at[:, :, 1:1 + size_x, 1 + size_y]  16.9 us
    ppermute x10, waiting for transfers between devices, extended(): lax.ppermute(lax.slice_in_dim(block, block.shape[dim] - width, None, axis...  16.2 us
    all_gather x1, blocking collectives, body(): lax.all_gather(states[1], 'mem', axis=0, tiled=True)  16.1 us
    all_gather x1, blocking collectives, body(): lax.all_gather(states[5], 'mem', axis=0, tiled=True)  15.8 us
    all_gather x1, blocking collectives, body(): lax.all_gather(states[2], 'mem', axis=0, tiled=True)  14.7 us
  transfers between devices with their start and end apart: 20, of which 8 were waited for; matrix products, arithmetic and copies ran while one was open for 9% of the time, Pallas kernels for 0%

profile of v1, /device:TPU:10, one launch (start us, length us, event | category | flops | bytes accessed | tf_op | source)
XLA Modules:
  0.0 237.1 jit_solution(6143085697636917998)
XLA Ops:
  1.5 1.7 collective-permute-start
  5.3 4.3 %collective-permute-start.16 = (f32[1,4,1,128]{3,1,2,0:T(4,128)S(1)}, f32[1,4,1,128]{3,1,2,0:T(4,128)S(1)}, u32[]{:S(2)}, u32[]{:S(2)}) collective-permute-start(f32[1,4,1,128]{3,1,2,0:T(4,128)S(1)} %copy.119), channel_id=1, source_target_pairs={{0,2},{2,4},{4,6},{1,3},{3,5},{5,7},{8,10},{10,12},{12,14},{9,11},... | collective-permute-start | bytes 6152 | tf_op jit(solution)/shard_map/ppermute | solution.py:17
  18.1 17.2 %all-gather = f32[128,384]{1,0:T(8,128)S(1)} all-gather(f32[16,384]{1,0:T(8,128)S(1)} %fusion.78), channel_id=2, replica_groups=mesh['mem'=4,'gx'=4,'gy'=2] {'gx','gy'}, dimensions={0}, use_global_device_ids=true | all-gather | bytes 221184 | tf_op jit(solution)/shard_map/all_gather | solution.py:82
  36.2 15.8 %all_gather.31 = f32[4,4,4,2048]{3,2,1,0:T(4,128)S(1)} all-gather(f32[1,4,4,2048]{3,2,1,0:T(4,128)S(1)} %get-tuple-element.293), channel_id=1, replica_groups=mesh['mem'=4,'gx'=4,'gy'=2] {'mem'}, dimensions={0}, use_global_device_ids=true | all-gather | bytes 655360 | tf_op jit(solution)/shard_map/all_gather | solution.py:169
  54.6 3.6 %collective-permute-start.3 = (f32[1,4,34,1]{3,1,2,0:T(4,128)S(1)}, f32[1,4,34,1]{3,1,2,0:T(4,128)S(1)}, u32[]{:S(2)}, u32[]{:S(2)}) collective-permute-start(f32[1,4,34,1]{3,1,2,0:T(4,128)S(1)} %get-tuple-element.271), channel_id=1, source_target_pairs={{1,0},{3,2},{5,4},{7,6},{9,8},{11,10},{13,12},{15,14},{17,16},{19,... | collective-permute-start | bytes 1640 | tf_op jit(solution)/shard_map/ppermute | solution.py:20
  60.2 4.3 %collective-permute-done.2 = f32[1,4,34,1]{3,1,2,0:T(4,128)S(1)} collective-permute-done((f32[1,4,34,1]{3,1,2,0:T(4,128)S(1)}, f32[1,4,34,1]{3,1,2,0:T(4,128)S(1)}, u32[]{:S(2)}, u32[]{:S(2)}) %collective-permute-start.2) | collective-permute-done | bytes 576 | tf_op jit(solution)/shard_map/ppermute | solution.py:17
  64.6 1.5 scatter.66
  67.2 2.4 %scatter.71 = f32[4,34,130]{2,0,1:T(4,128)S(1)} dynamic-update-slice(f32[4,34,130]{2,0,1:T(4,128)S(1)} %bitcast.151, f32[4,32,1]{2,0,1:T(4,128)S(1)} %copy.81, s32[]{:T(128)} %constant.509.clone.1, s32[]{:T(128)} %constant.517.clone.1, s32[]{:T(128)} %constant.523.clone.1) | dynamic-update-slice | bytes 1028 | tf_op jit(solution)/shard_map/scatter | solution.py:44
  71.1 3.0 %collective-permute-start.4 = (f32[2,4,1,128]{3,1,2,0:T(4,128)S(1)}, f32[2,4,1,128]{3,1,2,0:T(4,128)S(1)}, u32[]{:S(2)}, u32[]{:S(2)}) collective-permute-start(f32[2,4,1,128]{3,1,2,0:T(4,128)S(1)} %get-tuple-element.262), channel_id=1, source_target_pairs={{0,2},{2,4},{4,6},{1,3},{3,5},{5,7},{8,10},{10,12},{12,14},{9,11},... | collective-permute-start | bytes 12296 | tf_op jit(solution)/shard_map/ppermute | solution.py:17
  74.2 1.6 collective-permute-start.19
  77.3 4.6 %collective-permute-start.7 = (f32[2,4,34,1]{3,1,2,0:T(4,128)S(1)}, f32[2,4,34,1]{3,1,2,0:T(4,128)S(1)}, u32[]{:S(2)}, u32[]{:S(2)}) collective-permute-start(f32[2,4,34,1]{3,1,2,0:T(4,128)S(1)} %get-tuple-element.257), channel_id=1, source_target_pairs={{1,0},{3,2},{5,4},{7,6},{9,8},{11,10},{13,12},{15,14},{17,16},{19,... | collective-permute-start | bytes 3272 | tf_op jit(solution)/shard_map/ppermute | solution.py:20
  83.2 2.6 %collective-permute-done.7 = f32[2,4,34,1]{3,1,2,0:T(4,128)S(1)} collective-permute-done((f32[2,4,34,1]{3,1,2,0:T(4,128)S(1)}, f32[2,4,34,1]{3,1,2,0:T(4,128)S(1)}, u32[]{:S(2)}, u32[]{:S(2)}) %collective-permute-start.7) | collective-permute-done | bytes 1120 | tf_op jit(solution)/shard_map/ppermute | solution.py:20
  85.8 4.1 %collective-permute-done.6 = f32[2,4,34,1]{3,1,2,0:T(4,128)S(1)} collective-permute-done((f32[2,4,34,1]{3,1,2,0:T(4,128)S(1)}, f32[2,4,34,1]{3,1,2,0:T(4,128)S(1)}, u32[]{:S(2)}, u32[]{:S(2)}) %collective-permute-start.6) | collective-permute-done | bytes 1120 | tf_op jit(solution)/shard_map/ppermute | solution.py:17
  90.2 1.6 scatter.74
  93.0 4.8 %scatter.79 = f32[2,4,34,130]{3,1,2,0:T(4,128)S(1)} dynamic-update-slice(f32[2,4,34,130]{3,1,2,0:T(4,128)S(1)} %scatter.76, f32[2,4,32,1]{3,1,2,0:T(4,128)S(1)} %slice_select_fusion.2, s32[]{:T(128)} %constant.509.clone.1, s32[]{:T(128)} %constant.509.clone.1, s32[]{:T(128)} %constant.517.clone.1, s32[]{:T(128)} %constant.523.clone.1) | dynamic-update-slice | bytes 2052 | tf_op jit(solution)/shard_map/scatter | solution.py:44
  98.0 1.6 collective-permute-start.8
  101.2 2.1 collective-permute-done.9
  107.7 3.4 %collective-permute-done.10 = f32[1,4,34,1]{3,1,2,0:T(4,128)S(1)} collective-permute-done((f32[1,4,34,1]{3,1,2,0:T(4,128)S(1)}, f32[1,4,34,1]{3,1,2,0:T(4,128)S(1)}, u32[]{:S(2)}, u32[]{:S(2)}) %collective-permute-start.10) | collective-permute-done | bytes 576 | tf_op jit(solution)/shard_map/ppermute | solution.py:17
  114.9 2.4 %scatter.99 = f32[4,34,130]{2,0,1:T(4,128)S(1)} dynamic-update-slice(f32[4,34,130]{2,0,1:T(4,128)S(1)} %bitcast.149, f32[4,32,1]{2,0,1:T(4,128)S(1)} %copy.100, s32[]{:T(128)} %constant.509.clone.1, s32[]{:T(128)} %constant.517.clone.1, s32[]{:T(128)} %constant.523.clone.1) | dynamic-update-slice | bytes 1028 | tf_op jit(solution)/shard_map/scatter | solution.py:44
  117.3 2.6 %scatter.85 = f32[4,34,130]{2,0,1:T(4,128)S(1)} dynamic-update-slice(f32[4,34,130]{2,0,1:T(4,128)S(1)} %bitcast.150, f32[4,32,1]{2,0,1:T(4,128)S(1)} %copy.88, s32[]{:T(128)} %constant.509.clone.1, s32[]{:T(128)} %constant.517.clone.1, s32[]{:T(128)} %constant.523.clone.1) | dynamic-update-slice | bytes 1028 | tf_op jit(solution)/shard_map/scatter | solution.py:44
  121.6 3.5 %collective-permute-start.12 = (f32[2,4,1,128]{3,1,2,0:T(4,128)S(1)}, f32[2,4,1,128]{3,1,2,0:T(4,128)S(1)}, u32[]{:S(2)}, u32[]{:S(2)}) collective-permute-start(f32[2,4,1,128]{3,1,2,0:T(4,128)S(1)} %get-tuple-element.260), channel_id=1, source_target_pairs={{0,2},{2,4},{4,6},{1,3},{3,5},{5,7},{8,10},{10,12},{12,14},{9,11},... | collective-permute-start | bytes 12296 | tf_op jit(solution)/shard_map/ppermute | solution.py:17
  125.1 16.1 %all-gather.2 = f32[8,4,32,128]{3,2,1,0:T(8,128)S(1)} all-gather(f32[2,4,32,128]{3,2,1,0:T(8,128)S(1)} %copy.92), channel_id=4, replica_groups=mesh['mem'=4,'gx'=4,'gy'=2] {'mem'}, dimensions={0}, use_global_device_ids=true | all-gather | bytes 655360 | tf_op jit(solution)/shard_map/all_gather | solution.py:165
  142.0 14.7 %all-gather.3 = f32[16,32,128]{2,1,0:T(8,128)S(1)} all-gather(f32[4,32,128]{2,1,0:T(8,128)S(1)} %copy.101), channel_id=5, replica_groups=mesh['mem'=4,'gx'=4,'gy'=2] {'mem'}, dimensions={0}, use_global_device_ids=true | all-gather | bytes 327680 | tf_op jit(solution)/shard_map/all_gather | solution.py:166
  157.4 13.2 %all-gather.4 = f32[128,128]{1,0:T(8,128)S(1)} all-gather(f32[32,128]{1,0:T(8,128)S(1)} %get-tuple-element.246), channel_id=6, replica_groups=mesh['mem'=4,'gx'=4,'gy'=2] {'mem'}, dimensions={0}, use_global_device_ids=true | all-gather | bytes 81920 | tf_op jit(solution)/shard_map/all_gather | solution.py:167
  170.9 7.0 %psum.14 = f32[4,16,32]{2,1,0:T(8,128)S(1)} all-reduce(f32[4,16,32]{2,1,0:T(8,128)S(1)} %fusion.36), channel_id=1, replica_groups=mesh['mem'=4,'gx'=4,'gy'=2] {'gy'}, use_global_device_ids=true, to_apply=%region_2.3 | all-reduce | flops 2048 | bytes 16384 | tf_op jit(solution)/shard_map/psum | solution.py:151
  177.9 10.3 %psum.15 = f32[4,16,32]{2,1,0:T(8,128)S(1)} all-reduce(f32[4,16,32]{2,1,0:T(8,128)S(1)} %psum.14), channel_id=1, replica_groups=mesh['mem'=4,'gx'=4,'gy'=2] {'gx'}, use_global_device_ids=true, to_apply=%region_3.4 | all-reduce | flops 2048 | bytes 16384 | tf_op jit(solution)/shard_map/psum | solution.py:152
  188.2 13.6 %all-gather.5 = f32[16,16,32]{2,1,0:T(8,128)S(1)} all-gather(f32[4,16,32]{2,1,0:T(8,128)S(1)} %broadcast_divide_fusion), channel_id=7, replica_groups=mesh['mem'=4,'gx'=4,'gy'=2] {'mem'}, dimensions={0}, use_global_device_ids=true | all-gather | bytes 40960 | tf_op jit(solution)/shard_map/all_gather | solution.py:168
  203.2 3.8 %collective-permute-start.15 = (f32[2,4,34,1]{3,1,2,0:T(4,128)S(1)}, f32[2,4,34,1]{3,1,2,0:T(4,128)S(1)}, u32[]{:S(2)}, u32[]{:S(2)}) collective-permute-start(f32[2,4,34,1]{3,1,2,0:T(4,128)S(1)} %get-tuple-element.255), channel_id=1, source_target_pairs={{1,0},{3,2},{5,4},{7,6},{9,8},{11,10},{13,12},{15,14},{17,16},{19,... | collective-permute-start | bytes 3272 | tf_op jit(solution)/shard_map/ppermute | solution.py:20
  209.6 4.4 %collective-permute-done.14 = f32[2,4,34,1]{3,1,2,0:T(4,128)S(1)} collective-permute-done((f32[2,4,34,1]{3,1,2,0:T(4,128)S(1)}, f32[2,4,34,1]{3,1,2,0:T(4,128)S(1)}, u32[]{:S(2)}, u32[]{:S(2)}) %collective-permute-start.14) | collective-permute-done | bytes 1120 | tf_op jit(solution)/shard_map/ppermute | solution.py:17
  214.2 1.6 scatter.86
  217.0 4.8 %scatter.91 = f32[2,4,34,130]{3,1,2,0:T(4,128)S(1)} dynamic-update-slice(f32[2,4,34,130]{3,1,2,0:T(4,128)S(1)} %scatter.90, f32[2,4,32,1]{3,1,2,0:T(4,128)S(1)} %slice_select_fusion, s32[]{:T(128)} %constant.509.clone.1, s32[]{:T(128)} %constant.509.clone.1, s32[]{:T(128)} %constant.517.clone.1, s32[]{:T(128)} %constant.523.clone.1) | dynamic-update-slice | bytes 2052 | tf_op jit(solution)/shard_map/scatter | solution.py:44
  222.0 14.4 %all-gather.1 = f32[16,32,128]{2,1,0:T(8,128)S(1)} all-gather(f32[4,32,128]{2,1,0:T(8,128)S(1)} %copy.91), channel_id=3, replica_groups=mesh['mem'=4,'gx'=4,'gy'=2] {'mem'}, dimensions={0}, use_global_device_ids=true | all-gather | bytes 327680 | tf_op jit(solution)/shard_map/all_gather | solution.py:164
  (158 shorter events, 40.8 us)
Async XLA Ops:
  0.6 17.1 %copy-start = (bf16[2048,384]{1,0:T(8,128)(2,1)S(1)}, bf16[2048,384]{1,0:T(8,128)(2,1)}, u32[]{:S(2)}) copy-start(bf16[2048,384]{1,0:T(8,128)(2,1)} %param.59) | copy-start | bytes 4718596
  0.6 34.6 %copy-start.6 = (s32[768]{0:T(1024)S(1)}, s32[768]{0:T(1024)}, u32[]{:S(2)}) copy-start(s32[768]{0:T(1024)} %param.60) | copy-start | bytes 9220
  0.7 35.6 %copy-start.3 = (f32[1,2,4,32,128]{4,3,2,1,0:T(8,128)S(1)}, f32[1,2,4,32,128]{4,3,2,1,0:T(8,128)}, u32[]{:S(2)}) copy-start(f32[1,2,4,32,128]{4,3,2,1,0:T(8,128)} %param.54) | copy-start | bytes 393220
  1.5 52.8 %collective-permute-start = (f32[1,4,1,128]{3,1,2,0:T(4,128)S(1)}, f32[1,4,1,128]{3,1,2,0:T(4,128)S(1)}, u32[]{:S(2)}, u32[]{:S(2)}) collective-permute-start(f32[1,4,1,128]{3,1,2,0:T(4,128)S(1)} %copy.117), channel_id=1, source_target_pairs={{0,2},{2,4},{4,6},{1,3},{3,5},{5,7},{8,10},{10,12},{12,14},{9,11},... | collective-permute-start | bytes 6152 | tf_op jit(solution)/shard_map/ppermute | solution.py:17
  3.3 51.2 %collective-permute-start.1 = (f32[1,4,1,128]{3,1,2,0:T(4,128)S(1)}, f32[1,4,1,128]{3,1,2,0:T(4,128)S(1)}, u32[]{:S(2)}, u32[]{:S(2)}) collective-permute-start(f32[1,4,1,128]{3,1,2,0:T(4,128)S(1)} %copy.118), channel_id=1, source_target_pairs={{2,0},{4,2},{6,4},{3,1},{5,3},{7,5},{10,8},{12,10},{14,12},{11,9},... | collective-permute-start | bytes 6152 | tf_op jit(solution)/shard_map/ppermute | solution.py:20
  5.3 54.2 %collective-permute-start.16 = (f32[1,4,1,128]{3,1,2,0:T(4,128)S(1)}, f32[1,4,1,128]{3,1,2,0:T(4,128)S(1)}, u32[]{:S(2)}, u32[]{:S(2)}) collective-permute-start(f32[1,4,1,128]{3,1,2,0:T(4,128)S(1)} %copy.119), channel_id=1, source_target_pairs={{0,2},{2,4},{4,6},{1,3},{3,5},{5,7},{8,10},{10,12},{12,14},{9,11},... | collective-permute-start | bytes 6152 | tf_op jit(solution)/shard_map/ppermute | solution.py:17
  9.7 50.0 %collective-permute-start.17 = (f32[1,4,1,128]{3,1,2,0:T(4,128)S(1)}, f32[1,4,1,128]{3,1,2,0:T(4,128)S(1)}, u32[]{:S(2)}, u32[]{:S(2)}) collective-permute-start(f32[1,4,1,128]{3,1,2,0:T(4,128)S(1)} %copy.120), channel_id=1, source_target_pairs={{2,0},{4,2},{6,4},{3,1},{5,3},{7,5},{10,8},{12,10},{14,12},{11,9},... | collective-permute-start | bytes 6152 | tf_op jit(solution)/shard_map/ppermute | solution.py:20
  17.8 36.6 %copy-start.2 = (f32[1,4,32,128]{3,2,1,0:T(8,128)S(1)}, f32[1,4,32,128]{3,2,1,0:T(8,128)}, u32[]{:S(2)}) copy-start(f32[1,4,32,128]{3,2,1,0:T(8,128)} %param.53) | copy-start | bytes 196612
  18.1 41.5 %copy-start.1 = (f32[1,4,32,128]{3,2,1,0:T(8,128)S(1)}, f32[1,4,32,128]{3,2,1,0:T(8,128)}, u32[]{:S(2)}) copy-start(f32[1,4,32,128]{3,2,1,0:T(8,128)} %param.55) | copy-start | bytes 196612
  54.6 5.6 %collective-permute-start.3 = (f32[1,4,34,1]{3,1,2,0:T(4,128)S(1)}, f32[1,4,34,1]{3,1,2,0:T(4,128)S(1)}, u32[]{:S(2)}, u32[]{:S(2)}) collective-permute-start(f32[1,4,34,1]{3,1,2,0:T(4,128)S(1)} %get-tuple-element.271), channel_id=1, source_target_pairs={{1,0},{3,2},{5,4},{7,6},{9,8},{11,10},{13,12},{15,14},{17,16},{19,... | collective-permute-start | bytes 1640 | tf_op jit(solution)/shard_map/ppermute | solution.py:20
  58.2 6.2 %collective-permute-start.2 = (f32[1,4,34,1]{3,1,2,0:T(4,128)S(1)}, f32[1,4,34,1]{3,1,2,0:T(4,128)S(1)}, u32[]{:S(2)}, u32[]{:S(2)}) collective-permute-start(f32[1,4,34,1]{3,1,2,0:T(4,128)S(1)} %get-tuple-element.270), channel_id=1, source_target_pairs={{0,1},{2,3},{4,5},{6,7},{8,9},{10,11},{12,13},{14,15},{16,17},{18,... | collective-permute-start | bytes 1640 | tf_op jit(solution)/shard_map/ppermute | solution.py:17
  69.8 7.3 %collective-permute-start.5 = (f32[2,4,1,128]{3,1,2,0:T(4,128)S(1)}, f32[2,4,1,128]{3,1,2,0:T(4,128)S(1)}, u32[]{:S(2)}, u32[]{:S(2)}) collective-permute-start(f32[2,4,1,128]{3,1,2,0:T(4,128)S(1)} %get-tuple-element.263), channel_id=1, source_target_pairs={{2,0},{4,2},{6,4},{3,1},{5,3},{7,5},{10,8},{12,10},{14,12},{11,9},... | collective-permute-start | bytes 12296 | tf_op jit(solution)/shard_map/ppermute | solution.py:20
  71.1 6.0 %collective-permute-start.4 = (f32[2,4,1,128]{3,1,2,0:T(4,128)S(1)}, f32[2,4,1,128]{3,1,2,0:T(4,128)S(1)}, u32[]{:S(2)}, u32[]{:S(2)}) collective-permute-start(f32[2,4,1,128]{3,1,2,0:T(4,128)S(1)} %get-tuple-element.262), channel_id=1, source_target_pairs={{0,2},{2,4},{4,6},{1,3},{3,5},{5,7},{8,10},{10,12},{12,14},{9,11},... | collective-permute-start | bytes 12296 | tf_op jit(solution)/shard_map/ppermute | solution.py:17
  74.2 26.7 %collective-permute-start.19 = (f32[1,4,34,1]{3,1,2,0:T(4,128)S(1)}, f32[1,4,34,1]{3,1,2,0:T(4,128)S(1)}, u32[]{:S(2)}, u32[]{:S(2)}) collective-permute-start(f32[1,4,34,1]{3,1,2,0:T(4,128)S(1)} %get-tuple-element.267), channel_id=1, source_target_pairs={{1,0},{3,2},{5,4},{7,6},{9,8},{11,10},{13,12},{15,14},{17,16},{19,... | collective-permute-start | bytes 1640 | tf_op jit(solution)/shard_map/ppermute | solution.py:20
  75.8 25.2 %collective-permute-start.18 = (f32[1,4,34,1]{3,1,2,0:T(4,128)S(1)}, f32[1,4,34,1]{3,1,2,0:T(4,128)S(1)}, u32[]{:S(2)}, u32[]{:S(2)}) collective-permute-start(f32[1,4,34,1]{3,1,2,0:T(4,128)S(1)} %get-tuple-element.266), channel_id=1, source_target_pairs={{0,1},{2,3},{4,5},{6,7},{8,9},{10,11},{12,13},{14,15},{16,17},{18,... | collective-permute-start | bytes 1640 | tf_op jit(solution)/shard_map/ppermute | solution.py:17
  77.3 8.5 %collective-permute-start.7 = (f32[2,4,34,1]{3,1,2,0:T(4,128)S(1)}, f32[2,4,34,1]{3,1,2,0:T(4,128)S(1)}, u32[]{:S(2)}, u32[]{:S(2)}) collective-permute-start(f32[2,4,34,1]{3,1,2,0:T(4,128)S(1)} %get-tuple-element.257), channel_id=1, source_target_pairs={{1,0},{3,2},{5,4},{7,6},{9,8},{11,10},{13,12},{15,14},{17,16},{19,... | collective-permute-start | bytes 3272 | tf_op jit(solution)/shard_map/ppermute | solution.py:20
  81.9 8.1 %collective-permute-start.6 = (f32[2,4,34,1]{3,1,2,0:T(4,128)S(1)}, f32[2,4,34,1]{3,1,2,0:T(4,128)S(1)}, u32[]{:S(2)}, u32[]{:S(2)}) collective-permute-start(f32[2,4,34,1]{3,1,2,0:T(4,128)S(1)} %get-tuple-element.256), channel_id=1, source_target_pairs={{0,1},{2,3},{4,5},{6,7},{8,9},{10,11},{12,13},{14,15},{16,17},{18,... | collective-permute-start | bytes 3272 | tf_op jit(solution)/shard_map/ppermute | solution.py:17
  97.8 22.1 %copy-start.4 = (f32[4]{0:T(128)S(1)}, f32[4]{0:T(128)}, u32[]{:S(2)}) copy-start(f32[4]{0:T(128)} %param.64) | copy-start | bytes 52
  97.8 22.1 %copy-start.5 = (f32[4]{0:T(128)S(1)}, f32[4]{0:T(128)}, u32[]{:S(2)}) copy-start(f32[4]{0:T(128)} %param.63) | copy-start | bytes 52
  98.0 3.1 %collective-permute-start.8 = (f32[1,4,1,128]{3,1,2,0:T(4,128)S(1)}, f32[1,4,1,128]{3,1,2,0:T(4,128)S(1)}, u32[]{:S(2)}, u32[]{:S(2)}) collective-permute-start(f32[1,4,1,128]{3,1,2,0:T(4,128)S(1)} %get-tuple-element.274), channel_id=1, source_target_pairs={{0,2},{2,4},{4,6},{1,3},{3,5},{5,7},{8,10},{10,12},{12,14},{9,11},... | collective-permute-start | bytes 6152 | tf_op jit(solution)/shard_map/ppermute | solution.py:17
  99.7 3.6 %collective-permute-start.9 = (f32[1,4,1,128]{3,1,2,0:T(4,128)S(1)}, f32[1,4,1,128]{3,1,2,0:T(4,128)S(1)}, u32[]{:S(2)}, u32[]{:S(2)}) collective-permute-start(f32[1,4,1,128]{3,1,2,0:T(4,128)S(1)} %get-tuple-element.275), channel_id=1, source_target_pairs={{2,0},{4,2},{6,4},{3,1},{5,3},{7,5},{10,8},{12,10},{14,12},{11,9},... | collective-permute-start | bytes 6152 | tf_op jit(solution)/shard_map/ppermute | solution.py:20
  103.4 4.3 %collective-permute-start.11 = (f32[1,4,34,1]{3,1,2,0:T(4,128)S(1)}, f32[1,4,34,1]{3,1,2,0:T(4,128)S(1)}, u32[]{:S(2)}, u32[]{:S(2)}) collective-permute-start(f32[1,4,34,1]{3,1,2,0:T(4,128)S(1)} %get-tuple-element.269), channel_id=1, source_target_pairs={{1,0},{3,2},{5,4},{7,6},{9,8},{11,10},{13,12},{15,14},{17,16},{19,... | collective-permute-start | bytes 1640 | tf_op jit(solution)/shard_map/ppermute | solution.py:20
  104.9 6.2 %collective-permute-start.10 = (f32[1,4,34,1]{3,1,2,0:T(4,128)S(1)}, f32[1,4,34,1]{3,1,2,0:T(4,128)S(1)}, u32[]{:S(2)}, u32[]{:S(2)}) collective-permute-start(f32[1,4,34,1]{3,1,2,0:T(4,128)S(1)} %get-tuple-element.268), channel_id=1, source_target_pairs={{0,1},{2,3},{4,5},{6,7},{8,9},{10,11},{12,13},{14,15},{16,17},{18,... | collective-permute-start | bytes 1640 | tf_op jit(solution)/shard_map/ppermute | solution.py:17
  120.3 82.7 %collective-permute-start.13 = (f32[2,4,1,128]{3,1,2,0:T(4,128)S(1)}, f32[2,4,1,128]{3,1,2,0:T(4,128)S(1)}, u32[]{:S(2)}, u32[]{:S(2)}) collective-permute-start(f32[2,4,1,128]{3,1,2,0:T(4,128)S(1)} %get-tuple-element.261), channel_id=1, source_target_pairs={{2,0},{4,2},{6,4},{3,1},{5,3},{7,5},{10,8},{12,10},{14,12},{11,9},... | collective-permute-start | bytes 12296 | tf_op jit(solution)/shard_map/ppermute | solution.py:20
  121.6 81.4 %collective-permute-start.12 = (f32[2,4,1,128]{3,1,2,0:T(4,128)S(1)}, f32[2,4,1,128]{3,1,2,0:T(4,128)S(1)}, u32[]{:S(2)}, u32[]{:S(2)}) collective-permute-start(f32[2,4,1,128]{3,1,2,0:T(4,128)S(1)} %get-tuple-element.260), channel_id=1, source_target_pairs={{0,2},{2,4},{4,6},{1,3},{3,5},{5,7},{8,10},{10,12},{12,14},{9,11},... | collective-permute-start | bytes 12296 | tf_op jit(solution)/shard_map/ppermute | solution.py:17
  203.2 6.4 %collective-permute-start.15 = (f32[2,4,34,1]{3,1,2,0:T(4,128)S(1)}, f32[2,4,34,1]{3,1,2,0:T(4,128)S(1)}, u32[]{:S(2)}, u32[]{:S(2)}) collective-permute-start(f32[2,4,34,1]{3,1,2,0:T(4,128)S(1)} %get-tuple-element.255), channel_id=1, source_target_pairs={{1,0},{3,2},{5,4},{7,6},{9,8},{11,10},{13,12},{15,14},{17,16},{19,... | collective-permute-start | bytes 3272 | tf_op jit(solution)/shard_map/ppermute | solution.py:20
  207.0 6.9 %collective-permute-start.14 = (f32[2,4,34,1]{3,1,2,0:T(4,128)S(1)}, f32[2,4,34,1]{3,1,2,0:T(4,128)S(1)}, u32[]{:S(2)}, u32[]{:S(2)}) collective-permute-start(f32[2,4,34,1]{3,1,2,0:T(4,128)S(1)} %get-tuple-element.254), channel_id=1, source_target_pairs={{0,1},{2,3},{4,5},{6,7},{8,9},{10,11},{12,13},{14,15},{16,17},{18,... | collective-permute-start | bytes 3272 | tf_op jit(solution)/shard_map/ppermute | solution.py:17
